TPU v7x, 32 devices: a whole 2x2x4 slice. The times are simulated.
32 devices in a mesh: dom: 2 (over x), pair: 8 (over z, y), aux: 2 (over core).
Axes of the slice: x: 2, y: 2, z: 4, core: 2. Of those that a mesh axis runs over, the one named last changes fastest.
Arguments:
- three_index: bfloat16 [3072, 16, 512], P('aux', ('dom', 'pair')), parts along dimension 1, may hold values from -0.796875 to 0.796875
- metric: bfloat16 [6144, 3072], P(('dom', 'pair'), 'aux'), parts along dimension 0, as said below
- occ_energy: float32 [16], P('dom'), parts along dimension 0, may hold values from -2 to -0.4
- vir_energy: float32 [1024], P('dom'), parts along dimension 0, may hold values from 0.2 to 3
- pair_list: int32 [16, 3, 2], P('dom'), parts along dimension 0, may hold values from -1 to 7, as said below
Outputs:
- density: float32 [3072, 16, 512], P('aux', ('dom', 'pair')), parts along dimension 1
There are 2 independent parts, one for each index of `dom`. A program takes and returns all parts, laid end to end along the dimension named above; each array names one. Nothing has to cross between parts.
Inputs may be any that keep to these rules, and one draw needn't show every extreme that they name: metric is symmetric up to rounding. `pair_list`: row b lists pairs (b, (b + d) mod 8) for distinct d of 1 to 3, in any order of slots; unused slots hold -1 in both columns; every row lists at least one pair, and some row lists 3.
All inputs are finite; a program needn't handle non-finite values.
Results may differ from a plain program's by a relative error of at most 0.0034.
Values may be sent and summed in bfloat16 or wider, within the bound.
No kernel may reach another device: no remote copies, remote signals or barrier semaphores. Data moves between devices by JAX's collectives and lax.ppermute only.
A program may use at most 128 MiB of HBM per device.

v0:
```python
import jax
import jax.numpy as jnp
from jax import lax
from jax.sharding import PartitionSpec as P


def shifted(block, axis, distance):
    devices = range(lax.axis_size(axis))
    route = [((i - distance) % len(devices), i) for i in devices]
    return lax.ppermute(block, axis, route)


def pair_product(left_side, right_side):
    return jnp.einsum("qia,qjb->ijab", left_side, right_side, preferred_element_type=jnp.float32)


def skip_product(left_side, right_side):
    return jnp.zeros(
        (left_side.shape[1], right_side.shape[1], left_side.shape[2], right_side.shape[2]),
        jnp.float32,
    )


def own_contraction(mixed, right_side):
    return jnp.einsum("ijab,qjb->qia", mixed, right_side, preferred_element_type=jnp.float32)


def skip_own(mixed, right_side):
    return jnp.zeros((right_side.shape[0], mixed.shape[0], mixed.shape[2]), jnp.float32)


def partner_contraction(mixed, left_side):
    return jnp.einsum("ijab,qia->qjb", mixed, left_side, preferred_element_type=jnp.float32).astype(
        jnp.bfloat16
    )


def skip_partner(mixed, left_side):
    return jnp.zeros((left_side.shape[0], mixed.shape[1], mixed.shape[3]), jnp.bfloat16)


def local(three_index, metric, occ_energy, vir_energy, pair_list):
    slab_rows, orbitals, virtuals = three_index.shape
    flattened = three_index.reshape(slab_rows, orbitals * virtuals)
    stacked = lax.all_gather(flattened, "aux", axis=0, tiled=True)
    metric_half = lax.all_gather(metric, "pair", axis=0, tiled=True)
    fitted = lax.dot_general(
        metric_half, stacked, (((0,), (0,)), ((), ())), preferred_element_type=jnp.float32
    )
    coeffs = fitted.astype(jnp.bfloat16).reshape(slab_rows, orbitals, virtuals)
    pair_count = lax.axis_size("pair")
    my_block = lax.axis_index("pair")
    farthest = pair_list.shape[1]
    listed = lax.dynamic_index_in_dim(pair_list, my_block, 0, keepdims=False)[:, 1]
    own_energy = lax.dynamic_slice_in_dim(occ_energy, my_block * orbitals, orbitals)
    partners = [coeffs]
    energies = [own_energy]
    active_flags = [jnp.array(True)]
    for offset in range(1, farthest + 1):
        fetched = shifted(coeffs, "pair", -offset)
        target = (my_block + offset) % pair_count
        partners.append(fetched)
        energies.append(lax.dynamic_slice_in_dim(occ_energy, target * orbitals, orbitals))
        active_flags.append(jnp.any(listed == target))
    partials = []
    for offset in range(farthest + 1):
        if offset == 0:
            partials.append(pair_product(coeffs, partners[0]))
        else:
            partials.append(
                lax.cond(active_flags[offset], pair_product, skip_product, coeffs, partners[offset])
            )
    summed = lax.psum(jnp.stack(partials), "aux")
    density = jnp.zeros((slab_rows, orbitals, virtuals), jnp.float32)
    for offset in range(farthest + 1):
        denominator = (
            own_energy[:, None, None, None]
            + energies[offset][None, :, None, None]
            - vir_energy[None, None, :, None]
            - vir_energy[None, None, None, :]
        )
        amplitude = summed[offset] / denominator
        mixed = (2.0 * amplitude - jnp.swapaxes(amplitude, 2, 3)).astype(jnp.bfloat16)
        if offset == 0:
            density = own_contraction(mixed, partners[0])
        else:
            density = density + lax.cond(
                active_flags[offset], own_contraction, skip_own, mixed, partners[offset]
            )
            returned_term = lax.cond(
                active_flags[offset], partner_contraction, skip_partner, mixed, coeffs
            )
            arrived = shifted(returned_term, "pair", offset)
            density = density + arrived.astype(jnp.float32)
    return density


def solution(mesh):
    return jax.shard_map(
        local,
        mesh=mesh,
        in_specs=(
            P("aux", ("dom", "pair"), None),
            P(("dom", "pair"), "aux"),
            P("dom"),
            P("dom"),
            P("dom", None, None),
        ),
        out_specs=P("aux", ("dom", "pair"), None),
        check_vma=False,
    )
```

profile of v0, /device:TPU:0, one launch (start us, length us, event | category | flops | bytes accessed | tf_op | source)
XLA Modules:
  0.0 521.4 jit_solution(81717733190509503)
XLA Ops:
  6.5 0.7 all-gather.6.cloned.1.call-update
  8.1 15.7 %all-gather.6.cloned.1.call-done = bf16[3072,1,512]{2,0,1:T(8,128)(2,1)} async-done(((bf16[1536,1,512]{2,0,1:T(8,128)(2,1)}), bf16[3072,1,512]{2,0,1:T(8,128)(2,1)}) %all-gather.6.cloned.1.call-update) | async-done | bytes 3145744 | tf_op jit(solution)/shard_map/all_gather | solution.py:45
  23.8 140.6 %all-gather.4.cloned.1.call-done = bf16[3072,1536]{1,0:T(8,128)(2,1)} async-done(((bf16[384,1536]{1,0:T(8,128)(2,1)}), bf16[3072,1536]{1,0:T(8,128)(2,1)}) %all-gather.4.cloned.1.call-update) | async-done | bytes 9437200 | tf_op jit(solution)/shard_map/all_gather | solution.py:46
  164.4 9.5 %fusion.41 = bf16[1536,512]{1,0:T(8,128)(2,1)S(1)} fusion(bf16[3072,1536]{1,0:T(8,128)(2,1)} %all-gather.4.cloned.1.call-done, bf16[3072,1,512]{2,0,1:T(8,128)(2,1)} %all-gather.6.cloned.1.call-done), kind=kOutput, calls=%fused_computation.38 | convolution fusion | flops 4832624640 | bytes 14155776 | tf_op jit(solution)/shard_map/dot_general | solution.py:47
  173.9 1.5 collective-permute-start.1
  175.4 1.6 collective-permute-start
  177.2 0.7 compare_reduce_fusion.2
  179.8 2.0 convolution_bitcast_fusion.4
  181.8 29.4 %collective-permute-done.1 = bf16[1536,1,512]{2,0,1:T(8,128)(2,1)S(1)} collective-permute-done((bf16[1536,1,512]{2,0,1:T(8,128)(2,1)S(1)}, bf16[1536,1,512]{2,0,1:T(8,128)(2,1)S(1)}, u32[]{:S(2)}, u32[]{:S(2)}) %collective-permute-start.1) | collective-permute-done | bytes 1572896 | tf_op jit(solution)/shard_map/ppermute | solution.py:10
  211.2 1.1 copy-done.5
  212.4 3.6 conditional.10
  212.4 1.2 copy-done.6
  213.6 2.4 fusion.11
  216.0 29.2 %collective-permute-done = bf16[1536,1,512]{2,0,1:T(8,128)(2,1)} collective-permute-done((bf16[1536,1,512]{2,0,1:T(8,128)(2,1)S(1)}, bf16[1536,1,512]{2,0,1:T(8,128)(2,1)}, u32[]{:S(2)}, u32[]{:S(2)}) %collective-permute-start) | collective-permute-done | bytes 1572896 | tf_op jit(solution)/shard_map/ppermute | solution.py:10
  245.1 3.4 conditional.9
  245.1 3.4 fusion.3
  248.5 28.0 %collective-permute-done.2 = bf16[1536,1,512]{2,0,1:T(8,128)(2,1)} collective-permute-done((bf16[1536,1,512]{2,0,1:T(8,128)(2,1)S(1)}, bf16[1536,1,512]{2,0,1:T(8,128)(2,1)}, u32[]{:S(2)}, u32[]{:S(2)}) %collective-permute-start.2) | collective-permute-done | bytes 1572896 | tf_op jit(solution)/shard_map/ppermute | solution.py:10
  276.6 3.4 conditional.11
  276.6 3.4 fusion.19
  280.0 4.5 pad_maximum_fusion
  290.4 57.1 %all-reduce.2.cloned.1.call-done = f32[4,1,1,512,512]{3,4,2,1,0:T(8,128)} async-done(((f32[4,1,1,512,512]{3,4,2,1,0:T(8,128)}), f32[4,1,1,512,512]{3,4,2,1,0:T(8,128)}) %all-reduce.2.cloned.1.call-update) | async-done | bytes 4194320 | tf_op jit(solution)/shard_map/psum | solution.py:73
  347.5 4.5 fusion.47
  352.0 2.6 copy.26
  354.6 2.6 fusion.50
  357.2 3.2 conditional.13
  357.2 3.2 fusion.26
  360.4 2.6 copy.27
  363.0 1.3 copy.28
  364.3 3.2 fusion.48
  367.5 3.2 conditional.15
  367.5 3.2 fusion.31
  370.7 1.3 collective-permute-start.4
  372.0 2.1 conditional.17
  372.0 2.1 fusion.36
  374.2 1.5 collective-permute-start.5
  375.7 1.3 copy.25
  377.0 4.2 conditional.12
  377.0 4.2 convolution_bitcast_fusion
  381.2 4.2 conditional.14
  381.2 4.2 convolution_bitcast_fusion.1
  385.4 4.1 conditional.16
  385.4 4.1 convolution_bitcast_fusion.2
  389.5 2.5 convolution_bitcast_fusion.3
  392.0 8.8 %collective-permute-done.3 = bf16[1536,1,512]{2,0,1:T(8,128)(2,1)} collective-permute-done((bf16[1536,1,512]{2,0,1:T(8,128)(2,1)}, bf16[1536,1,512]{2,0,1:T(8,128)(2,1)}, u32[]{:S(2)}, u32[]{:S(2)}) %collective-permute-start.3) | collective-permute-done | bytes 1572896 | tf_op jit(solution)/shard_map/ppermute | solution.py:10
  400.8 9.4 %collective-permute-done.4 = bf16[1536,1,512]{2,0,1:T(8,128)(2,1)} collective-permute-done((bf16[1536,1,512]{2,0,1:T(8,128)(2,1)}, bf16[1536,1,512]{2,0,1:T(8,128)(2,1)}, u32[]{:S(2)}, u32[]{:S(2)}) %collective-permute-start.4) | collective-permute-done | bytes 1572896 | tf_op jit(solution)/shard_map/ppermute | solution.py:10
  410.1 90.9 %collective-permute-done.5 = bf16[1536,1,512]{2,0,1:T(8,128)(2,1)} collective-permute-done((bf16[1536,1,512]{2,0,1:T(8,128)(2,1)}, bf16[1536,1,512]{2,0,1:T(8,128)(2,1)}, u32[]{:S(2)}, u32[]{:S(2)}) %collective-permute-start.5) | collective-permute-done | bytes 1572896 | tf_op jit(solution)/shard_map/ppermute | solution.py:10
  501.1 4.8 convert_add_fusion
  505.9 9.0 %copy.29 = f32[1536,1,512]{2,1,0:T(1,128)} copy(f32[1536,1,512]{2,0,1:T(8,128)S(1)} %convert_add_fusion) | data formatting | bytes 6291456 | tf_op jit(solution)/shard_map/add | solution.py:94
  (27 shorter events, 2.3 us)
Async XLA Ops:
  6.5 170.5 %copy-start = (s32[8,3,2]{0,2,1:T(2,128)S(1)}, s32[8,3,2]{0,2,1:T(2,128)}, u32[]{:S(2)}) copy-start(s32[8,3,2]{0,2,1:T(2,128)} %param.27) | copy-start | bytes 580
  6.5 17.2 %all-gather.6.cloned.1.call-start = ((), (), s32[]{:S(2)}) async-start(), calls=%async_computation.2 | async-start | bytes 4718592 | tf_op jit(solution)/shard_map/all_gather | solution.py:45
  7.3 157.1 %all-gather.4.cloned.1.call-start = ((), (), s32[]{:S(2)}) async-start(), calls=%async_computation | async-start | bytes 10616832 | tf_op jit(solution)/shard_map/all_gather | solution.py:46
  8.0 339.5 %all-reduce.2.cloned.1.call-start = ((), (), s32[]{:S(2)}) async-start(), calls=%async_computation.1 | async-start | bytes 8388608 | tf_op jit(solution)/shard_map/psum | solution.py:73
  173.9 37.3 %collective-permute-start.1 = (bf16[1536,1,512]{2,0,1:T(8,128)(2,1)S(1)}, bf16[1536,1,512]{2,0,1:T(8,128)(2,1)S(1)}, u32[]{:S(2)}, u32[]{:S(2)}) collective-permute-start(bf16[1536,1,512]{2,0,1:T(8,128)(2,1)S(1)} %bitcast.157), channel_id=1, source_target_pairs={{4,0},{6,2},{8,4},{10,6},{12,8},{14,10},{0,12},{2,14},{5,1},{7,3},... | collective-permute-start | bytes 4718600 | tf_op jit(solution)/shard_map/ppermute | solution.py:10
  175.4 69.8 %collective-permute-start = (bf16[1536,1,512]{2,0,1:T(8,128)(2,1)S(1)}, bf16[1536,1,512]{2,0,1:T(8,128)(2,1)}, u32[]{:S(2)}, u32[]{:S(2)}) collective-permute-start(bf16[1536,1,512]{2,0,1:T(8,128)(2,1)S(1)} %bitcast.158), channel_id=1, source_target_pairs={{2,0},{4,2},{6,4},{8,6},{10,8},{12,10},{14,12},{0,14},{3,1},{5,3},... | collective-permute-start | bytes 4718600 | tf_op jit(solution)/shard_map/ppermute | solution.py:10
  176.9 99.6 %collective-permute-start.2 = (bf16[1536,1,512]{2,0,1:T(8,128)(2,1)S(1)}, bf16[1536,1,512]{2,0,1:T(8,128)(2,1)}, u32[]{:S(2)}, u32[]{:S(2)}) collective-permute-start(bf16[1536,1,512]{2,0,1:T(8,128)(2,1)S(1)} %bitcast.159), channel_id=1, source_target_pairs={{6,0},{8,2},{10,4},{12,6},{14,8},{0,10},{2,12},{4,14},{7,1},{9,3},... | collective-permute-start | bytes 4718600 | tf_op jit(solution)/shard_map/ppermute | solution.py:10
  211.2 1.1 copy-start.5
  212.4 1.2 copy-start.6
  284.5 0.7 copy-start.7
  284.5 5.9 %copy-start.8 = (f32[512]{0:T(512)S(1)}, f32[512]{0:T(512)}, u32[]{:S(2)}) copy-start(f32[512]{0:T(512)} %param.26) | copy-start | bytes 6148
  360.4 40.4 %collective-permute-start.3 = (bf16[1536,1,512]{2,0,1:T(8,128)(2,1)}, bf16[1536,1,512]{2,0,1:T(8,128)(2,1)}, u32[]{:S(2)}, u32[]{:S(2)}) collective-permute-start(bf16[1536,1,512]{2,0,1:T(8,128)(2,1)} %get-tuple-element.128), channel_id=1, source_target_pairs={{14,0},{0,2},{2,4},{4,6},{6,8},{8,10},{10,12},{12,14},{15,1},{1,3}... | collective-permute-start | bytes 4718600 | tf_op jit(solution)/shard_map/ppermute | solution.py:10
  370.7 39.4 %collective-permute-start.4 = (bf16[1536,1,512]{2,0,1:T(8,128)(2,1)}, bf16[1536,1,512]{2,0,1:T(8,128)(2,1)}, u32[]{:S(2)}, u32[]{:S(2)}) collective-permute-start(bf16[1536,1,512]{2,0,1:T(8,128)(2,1)} %get-tuple-element.130), channel_id=1, source_target_pairs={{12,0},{14,2},{0,4},{2,6},{4,8},{6,10},{8,12},{10,14},{13,1},{15,3... | collective-permute-start | bytes 4718600 | tf_op jit(solution)/shard_map/ppermute | solution.py:10
  372.0 3.7 copy-start.4
  374.2 126.9 %collective-permute-start.5 = (bf16[1536,1,512]{2,0,1:T(8,128)(2,1)}, bf16[1536,1,512]{2,0,1:T(8,128)(2,1)}, u32[]{:S(2)}, u32[]{:S(2)}) collective-permute-start(bf16[1536,1,512]{2,0,1:T(8,128)(2,1)} %get-tuple-element.132), channel_id=1, source_target_pairs={{10,0},{12,2},{14,4},{0,6},{2,8},{4,10},{6,12},{8,14},{11,1},{13,3... | collective-permute-start | bytes 4718600 | tf_op jit(solution)/shard_map/ppermute | solution.py:10
  389.5 111.6 %copy-start.2 = (f32[1536,1,512]{2,0,1:T(8,128)S(1)}, f32[1536,1,512]{2,0,1:T(8,128)}, u32[]{:S(2)}) copy-start(f32[1536,1,512]{2,0,1:T(8,128)} %get-tuple-element.127) | copy-start | bytes 9437188
  389.5 111.6 %copy-start.3 = (f32[1536,1,512]{2,0,1:T(8,128)S(1)}, f32[1536,1,512]{2,0,1:T(8,128)}, u32[]{:S(2)}) copy-start(f32[1536,1,512]{2,0,1:T(8,128)} %get-tuple-element.129) | copy-start | bytes 9437188
  505.8 9.0 %copy-start.1 = (s32[8,3,2]{0,2,1:T(2,128)S(1)}, s32[8,3,2]{0,2,1:T(2,128)}, u32[]{:S(2)}) copy-start(s32[8,3,2]{0,2,1:T(2,128)} %param.27) | copy-start | bytes 580
Sparse Core Ops, SparseCore 0:
  8.9 14.8 all-gather.5
  25.9 138.4 all-gather.3
  284.7 62.7 all-reduce.1
where the time goes:
time: 522 us; the launch traced here: 521 us
  waiting for transfers between devices  411 us (79%)
  matrix products  44.2 us (8%)
  local copies, waits for them, and re-layouts  20.6 us (4%)
  other arithmetic  20.3 us (4%)
  between operations  19.7 us (4%)
  starting transfers between devices  5.98 us (1%)
    ppermute x6, waiting for transfers between devices, shifted(): return lax.ppermute(block, axis, route)  196 us
    all_gather x1, waiting for transfers between devices, local(): metric_half = lax.all_gather(metric, 'pair', axis=0, tiled=True)  141 us
    psum x1, waiting for transfers between devices, local(): summed = lax.psum(jnp.stack(partials), 'aux')  57.1 us
    all_gather x1, waiting for transfers between devices, local(): stacked = lax.all_gather(flattened, 'aux', axis=0, tiled=True)  15.7 us
    dot_general x4, matrix products, own_contraction(): jnp.einsum('ijab,qjb->qia', mixed, right_side, preferred_element_type=jnp...  14.9 us
    dot_general x4, matrix products, pair_product(): jnp.einsum('qia,qjb->ijab', left_side, right_side, preferred_element_type...  11.2 us
  transfers between devices with their start and end apart: 9, of which 9 were waited for; matrix products, arithmetic and copies ran while one was open for 7% of the time, Pallas kernels for 0%

commit v1 on v0

v1 whole, which is shorter than its diff:
```python
import jax
import jax.numpy as jnp
from jax import lax
from jax.sharding import PartitionSpec as P


def shifted(block, axis, distance):
    devices = range(lax.axis_size(axis))
    route = [((i - distance) % len(devices), i) for i in devices]
    return lax.ppermute(block, axis, route)


def swap_aux(x):
    return lax.ppermute(x, "aux", [(0, 1), (1, 0)])


def dot(x, y, cx, cy):
    return lax.dot_general(x, y, (((cx,), (cy,)), ((), ())), preferred_element_type=jnp.float32)


def ladder(orbital_block, metric, occ_energy, vir_energy, pair_list):
    slab_rows, _, virtuals = orbital_block.shape
    t_own = orbital_block.reshape(slab_rows, virtuals)
    count = lax.axis_size("pair")
    b = lax.axis_index("pair")
    core = lax.axis_index("aux")
    rung = b // 2
    inner = (rung == 1) | (rung == 2)
    right = (rung >= 2).astype(jnp.int32)
    rows = metric.shape[0]

    def send(x, route):
        return lax.ppermute(x, "pair", route)

    side_swap = [(p, p ^ 1) for p in range(count)]
    rung_swap = [(p, p ^ 2) for p in range(count)]
    mid = [(2, 4), (3, 5), (4, 2), (5, 3)]
    outward = [(2, 0), (3, 1), (4, 6), (5, 7)]

    def cores(route, which):
        return [(2 * s + which(s), 2 * d + which(s)) for s, d in route]

    def diag_core(p):
        return 0 if p < count // 2 else 1

    def far_core(p):
        return 1 - diag_core(p)

    def send_core(x, route, which):
        return lax.ppermute(x, ("pair", "aux"), cores(route, which))

    t_other = swap_aux(t_own)

    m_y = send(metric, side_swap)
    m_z = send(metric, rung_swap)
    far3i = send_core(metric, mid, diag_core)
    half = rows // 2
    far3o = send_core(far3i, outward, far_core)
    far4i = send_core(m_z, mid, diag_core)
    m_yz_top = send(m_z[:half], side_swap)
    m_yz_bot = send(m_y[half:], rung_swap)
    far4o = send_core(far4i, outward, far_core)
    far3 = jnp.where(inner, far3i, far3o)
    far4 = jnp.where(inner, far4i, far4o)
    far_swap = [(p, p ^ 1) for p in range(count)]
    far3y = send_core(far3, far_swap, far_core)
    far4y = send_core(far4, far_swap, far_core)
    m_yz = jnp.concatenate([m_yz_top, m_yz_bot], 0)

    near = [metric, m_y, m_z, m_yz]
    side = b % 2
    low = rung % 2

    def ordered(own, y, z, yz):
        e0 = jnp.where(side == 0, own, y)
        e1 = jnp.where(side == 0, y, own)
        g0 = jnp.where(side == 0, z, yz)
        g1 = jnp.where(side == 0, yz, z)
        return jnp.concatenate(
            [
                jnp.where(low == 0, e0, g0),
                jnp.where(low == 0, e1, g1),
                jnp.where(low == 0, g0, e0),
                jnp.where(low == 0, g1, e1),
            ],
            0,
        )

    block = ordered(*near)
    f3a = jnp.where(side == 0, far3, far3y)
    f3b = jnp.where(side == 0, far3y, far3)
    f4a = jnp.where(side == 0, far4, far4y)
    f4b = jnp.where(side == 0, far4y, far4)
    far_block = jnp.where(
        right == 0,
        jnp.concatenate([f3a, f3b, f4a, f4b], 0),
        jnp.concatenate([f4a, f4b, f3a, f3b], 0),
    )
    aux_route = [(2 * p + far_core(p), 2 * p + diag_core(p)) for p in range(count)]
    off_from = lax.ppermute(block, ("pair", "aux"), aux_route)
    on_diag = core == right
    diag = jnp.where(on_diag, block, far_block)
    off = jnp.where(on_diag, off_from, block)
    fitted = dot(diag, t_own, 0, 0) + lax.cond(
        on_diag, lambda o, t: dot(o, t, 1, 0), lambda o, t: dot(o, t, 0, 0), off, t_other
    )
    f = fitted.astype(jnp.bfloat16)

    f_y = send(f, side_swap)
    v2 = send(f, rung_swap)
    v3i = send(f, mid)
    v2_y = send(v2, side_swap)
    v3o = send(v3i, outward)
    v4i = send(v2, mid)
    v3 = jnp.where(inner, v3i, v3o)
    v3_y = send(v3, side_swap)
    v4o = send(v4i, outward)
    v4 = jnp.where(inner, v4i, v4o)
    v4_y = send(v4, side_swap)

    near_rung = rung ^ 1
    in_other = jnp.where(right == 0, 2, 1)
    out_other = jnp.where(right == 0, 3, 0)
    work = [
        (f, b),
        (f_y, b ^ 1),
        (v2, 2 * near_rung + side),
        (v2_y, 2 * near_rung + 1 - side),
        (v3, 2 * in_other + side),
        (v3_y, 2 * in_other + 1 - side),
        (v4, 2 * out_other + side),
        (v4_y, 2 * out_other + 1 - side),
    ]
    second = pair_list[:, :, 1]
    own_list = second[b]
    own_energy = occ_energy[b]
    vir_sum = vir_energy[:, None] + vir_energy[None, :]
    density = jnp.zeros((slab_rows, virtuals), jnp.float32)
    for g, j in work:
        partial = dot(f, g, 0, 0)
        total = partial + swap_aux(partial)
        amplitude = total / (own_energy + occ_energy[j] - vir_sum)
        listed = (j == b) | jnp.any(own_list == j) | jnp.any(second[j] == b)
        mixed = jnp.where(listed, 2.0 * amplitude - amplitude.T, 0.0).astype(jnp.bfloat16)
        density = density + dot(g, mixed, 1, 1)
    return density.reshape(slab_rows, 1, virtuals)


def pair_product(left_side, right_side):
    return jnp.einsum("qia,qjb->ijab", left_side, right_side, preferred_element_type=jnp.float32)


def ring(three_index, metric, occ_energy, vir_energy, pair_list):
    slab_rows, orbitals, virtuals = three_index.shape
    flattened = three_index.reshape(slab_rows, orbitals * virtuals)
    stacked = lax.all_gather(flattened, "aux", axis=0, tiled=True)
    metric_half = lax.all_gather(metric, "pair", axis=0, tiled=True)
    fitted = dot(metric_half, stacked, 0, 0)
    coeffs = fitted.astype(jnp.bfloat16).reshape(slab_rows, orbitals, virtuals)
    pair_count = lax.axis_size("pair")
    my_block = lax.axis_index("pair")
    farthest = pair_list.shape[1]
    listed = lax.dynamic_index_in_dim(pair_list, my_block, 0, keepdims=False)[:, 1]
    own_energy = lax.dynamic_slice_in_dim(occ_energy, my_block * orbitals, orbitals)
    density = jnp.zeros((slab_rows, orbitals, virtuals), jnp.float32)
    for offset in range(farthest + 1):
        target = (my_block + offset) % pair_count
        partner = shifted(coeffs, "pair", -offset) if offset else coeffs
        energy = lax.dynamic_slice_in_dim(occ_energy, target * orbitals, orbitals)
        active = jnp.any(listed == target) | (offset == 0)
        partial = pair_product(coeffs, partner)
        summed = lax.psum(partial, "aux")
        amplitude = summed / (
            own_energy[:, None, None, None]
            + energy[None, :, None, None]
            - vir_energy[None, None, :, None]
            - vir_energy[None, None, None, :]
        )
        mixed = jnp.where(active, 2.0 * amplitude - jnp.swapaxes(amplitude, 2, 3), 0.0)
        mixed = mixed.astype(jnp.bfloat16)
        density = density + jnp.einsum(
            "ijab,qjb->qia", mixed, partner, preferred_element_type=jnp.float32
        )
        if offset:
            term = jnp.einsum("ijab,qia->qjb", mixed, coeffs, preferred_element_type=jnp.float32)
            arrived = shifted(term.astype(jnp.bfloat16), "pair", offset)
            density = density + arrived.astype(jnp.float32)
    return density


def solution(mesh):
    def local(three_index, metric, occ_energy, vir_energy, pair_list):
        rungs = mesh.shape["pair"] // 2
        small = rungs == 4 and mesh.shape["aux"] == 2 and three_index.shape[1] == 1
        plan = ladder if small else ring
        return plan(three_index, metric, occ_energy, vir_energy, pair_list)

    return jax.shard_map(
        local,
        mesh=mesh,
        in_specs=(
            P("aux", ("dom", "pair"), None),
            P(("dom", "pair"), "aux"),
            P("dom"),
            P("dom"),
            P("dom", None, None),
        ),
        out_specs=P("aux", ("dom", "pair"), None),
        check_vma=False,
    )
```

time: 522 us -> 369 us (0.71)
  waiting for transfers between devices: 411 us -> 156 us
  starting transfers between devices: 5.98 us -> 69.8 us
  local copies, waits for them, and re-layouts: 20.6 us -> 38.3 us
  other arithmetic: 20.3 us -> 32.1 us
    all_gather x2 -> x0, waiting for transfers between devices: 156 us -> none  [the longest x1 141 us: local(): metric_half = lax.all_gather(metric, 'pair', axis=0, tiled=True)]
    ppermute x6 -> x29, starting transfers between devices: 5.9 us -> 69.8 us  [the longest x9 29.4 us: swap_aux(): return lax.ppermute(x, 'aux', [(0, 1), (1, 0)])]
    psum x1 -> x0, waiting for transfers between devices: 57.1 us -> none  [local(): summed = lax.psum(jnp.stack(partials), 'aux')]
    ppermute x6 -> x29, waiting for transfers between devices: 196 us -> 156 us  [the longest x13 156 us: send(): return lax.ppermute(x, 'pair', route)]
    select_n x0 -> x8, other arithmetic: none -> 18.6 us  [the longest x1 3.74 us: ladder(): off = jnp.where(on_diag, off_from, block)]
    div x4 -> x7, local copies, waits for them, and re-layouts: 7.86 us -> 17 us  [ladder(): amplitude = total / (own_energy + occ_energy[j] - vir_sum)]
    add x1 -> x0, local copies, waits for them, and re-layouts: 8.97 us -> none  [local(): density = density + arrived.astype(jnp.float32)]
    reshape x0 -> x1, local copies, waits for them, and re-layouts: none -> 8.97 us  [ladder(): return density.reshape(slab_rows, 1, virtuals)]
  transfers between devices with their start and end apart: 9 -> 29, of which waited for: 9 -> 8; matrix products, arithmetic and copies ran while one was open for 7% -> 20% of each run, Pallas kernels for 0% -> 0%
where the time goes in v1:
time: 369 us; the launch traced here: 365 us
  waiting for transfers between devices  156 us (42%)
  starting transfers between devices  69.8 us (19%)
  matrix products  49.3 us (13%)
  local copies, waits for them, and re-layouts  38.3 us (10%)
  other arithmetic  32.1 us (9%)
  between operations  19.4 us (5%)
    ppermute x13, waiting for transfers between devices, send(): return lax.ppermute(x, 'pair', route)  156 us
    dot_general x18, matrix products, dot(): lax.dot_general(x, y, (((cx,), (cy,)), ((), ())), preferred_element_type=...  49.3 us
    ppermute x9, starting transfers between devices, swap_aux(): return lax.ppermute(x, 'aux', [(0, 1), (1, 0)])  29.4 us
    ppermute x13, starting transfers between devices, send(): return lax.ppermute(x, 'pair', route)  29.1 us
    div x7, local copies, waits for them, and re-layouts, ladder(): amplitude = total / (own_energy + occ_energy[j] - vir_sum)  17 us
    ppermute x6, starting transfers between devices, send_core(): return lax.ppermute(x, ('pair', 'aux'), cores(route, which))  10.1 us
    reshape x1, local copies, waits for them, and re-layouts, ladder(): return density.reshape(slab_rows, 1, virtuals)  8.97 us
  transfers between devices with their start and end apart: 29, of which 8 were waited for; matrix products, arithmetic and copies ran while one was open for 20% of the time, Pallas kernels for 0%

profile of v1, /device:TPU:0, one launch (start us, length us, event | category | flops | bytes accessed | tf_op | source)
XLA Modules:
  0.0 364.9 jit_solution(497639344457993201)
XLA Ops:
  0.0 3.1 collective-permute-start.1
  4.6 24.7 %collective-permute-done.1 = bf16[384,1536]{1,0:T(8,128)(2,1)S(1)} collective-permute-done((bf16[384,1536]{1,0:T(8,128)(2,1)}, bf16[384,1536]{1,0:T(8,128)(2,1)S(1)}, u32[]{:S(2)}, u32[]{:S(2)}) %collective-permute-start.1) | collective-permute-done | bytes 1179680 | tf_op jit(solution)/shard_map/ppermute | solution.py:33
  30.1 1.7 collective-permute-start.2
  34.3 1.7 collective-permute-start.4
  36.0 8.9 %collective-permute-done.2 = bf16[192,1536]{1,0:T(8,128)(2,1)S(1)} collective-permute-done((bf16[192,1536]{1,0:T(8,128)(2,1)}, bf16[192,1536]{1,0:T(8,128)(2,1)S(1)}, u32[]{:S(2)}, u32[]{:S(2)}) %collective-permute-start.2) | collective-permute-done | bytes 589856 | tf_op jit(solution)/shard_map/ppermute | solution.py:33
  44.9 2.1 collective-permute-done.3
  48.4 2.0 broadcast_select_fusion.16
  50.5 2.6 pad_maximum_fusion
  54.6 1.7 collective-permute-start.7
  56.3 1.7 collective-permute-start.5
  58.0 1.7 collective-permute-start.8
  59.7 2.4 broadcast_select_fusion.4
  63.8 2.4 broadcast_select_fusion.3
  66.2 1.7 collective-permute-start.9
  67.9 28.2 %collective-permute-start.11 = (bf16[1536,512]{1,0:T(8,128)(2,1)}, bf16[1536,512]{1,0:T(8,128)(2,1)}, u32[]{:S(2)}, u32[]{:S(2)}) collective-permute-start(bf16[1536,512]{1,0:T(8,128)(2,1)} %bitcast), channel_id=1, source_target_pairs={{0,1},{1,0},{2,3},{3,2},{4,5},{5,4},{6,7},{7,6},{8,9},{9,8},{10,11... | collective-permute-start | bytes 4718600 | tf_op jit(solution)/shard_map/ppermute | solution.py:14
  96.1 3.2 broadcast_select_fusion.8
  99.3 3.3 broadcast_select_fusion.6
  102.6 3.7 %broadcast_select_fusion = bf16[1536,1536]{1,0:T(8,128)(2,1)S(1)} fusion(bf16[1536,1536]{1,0:T(8,128)(2,1)} %collective-permute-done.10, pred[]{:T(512)S(6)} %eq.140, bf16[384,1536]{1,0:T(8,128)(2,1)S(1)} %copy-done.10, bf16[384,1536]{1,0:T(8,128)(2,1)S(1)} %copy-done.8, bf16[384,1536]{1,0:T(8,128)(2,1)S(1)} %get-tuple-element.35, ...), kind=kLoop, calls=%fused_computation.18 | loop fusion | flops 21233664 | bytes 14155777 | tf_op jit(solution)/shard_map/jit(_where)/select_n | solution.py:103
  106.4 5.7 %conditional.1 = (f32[1536,512]{1,0:T(8,128)}) conditional(s32[]{:T(128)} %convert_element_type.34, (bf16[1536,1536]{1,0:T(8,128)(2,1)S(1)}, bf16[1536,512]{1,0:T(8,128)(2,1)}) %tuple.11, (bf16[1536,1536]{1,0:T(8,128)(2,1)S(1)}, bf16[1536,512]{1,0:T(8,128)(2,1)}) %tuple.11), branch_computations={%region_0.1_spmd, %region_1.2_spmd} | conditional | flops 2415919104 | bytes 9437192 | solution.py:104
  106.4 5.7 %fusion.103 = f32[1536,512]{1,0:T(8,128)} fusion(bf16[1536,1536]{1,0:T(8,128)(2,1)S(1)} %get-tuple-element.18, bf16[1536,512]{1,0:T(8,128)(2,1)} %get-tuple-element.19), kind=kOutput, calls=%fused_computation.153 | convolution fusion | flops 2415919104 | bytes 9437184 | tf_op jit(solution)/shard_map/cond/branch_1_fun/dot_general | solution.py:18
  112.1 7.7 %fusion.25 = bf16[1536,512]{1,0:T(8,128)(2,1)S(1)} fusion(f32[1536,512]{1,0:T(8,128)} %get-tuple-element.58, bf16[384,1536]{1,0:T(8,128)(2,1)} %get-tuple-element.41, bf16[384,1536]{1,0:T(8,128)(2,1)} %get-tuple-element.40, bf16[384,1536]{1,0:T(8,128)(2,1)} %get-tuple-element.39, bf16[384,1536]{1,0:T(8,128)(2,1)} %get-tuple-element.38, pred[]{:T(512)S(6)} %eq.143, ...), kind=kOutput, calls=%fused_computation.37 | convolution fusion | flops 2478833664 | bytes 15728642 | tf_op jit(solution)/shard_map/dot_general | solution.py:18
  120.5 13.8 %collective-permute-start.15 = (bf16[1536,512]{1,0:T(8,128)(2,1)S(1)}, bf16[1536,512]{1,0:T(8,128)(2,1)S(1)}, u32[]{:S(2)}, u32[]{:S(2)}) collective-permute-start(bf16[1536,512]{1,0:T(8,128)(2,1)S(1)} %fusion.25), channel_id=1, source_target_pairs={{0,4},{2,6},{4,0},{6,2},{8,12},{10,14},{12,8},{14,10},{1,5},{3,7},... | collective-permute-start | bytes 4718600 | tf_op jit(solution)/shard_map/ppermute | solution.py:33
  135.6 30.7 %collective-permute-done.15 = bf16[1536,512]{1,0:T(8,128)(2,1)S(1)} collective-permute-done((bf16[1536,512]{1,0:T(8,128)(2,1)S(1)}, bf16[1536,512]{1,0:T(8,128)(2,1)S(1)}, u32[]{:S(2)}, u32[]{:S(2)}) %collective-permute-start.15) | collective-permute-done | bytes 1572896 | tf_op jit(solution)/shard_map/ppermute | solution.py:33
  169.1 32.2 %collective-permute-done.20 = bf16[1536,512]{1,0:T(8,128)(2,1)S(1)} collective-permute-done((bf16[1536,512]{1,0:T(8,128)(2,1)S(1)}, bf16[1536,512]{1,0:T(8,128)(2,1)S(1)}, u32[]{:S(2)}, u32[]{:S(2)}) %collective-permute-start.20) | collective-permute-done | bytes 1572896 | tf_op jit(solution)/shard_map/ppermute | solution.py:33
  207.1 31.0 %collective-permute-done.17 = bf16[1536,512]{1,0:T(8,128)(2,1)S(1)} collective-permute-done((bf16[1536,512]{1,0:T(8,128)(2,1)S(1)}, bf16[1536,512]{1,0:T(8,128)(2,1)S(1)}, u32[]{:S(2)}, u32[]{:S(2)}) %collective-permute-start.17) | collective-permute-done | bytes 1572896 | tf_op jit(solution)/shard_map/ppermute | solution.py:33
  238.1 2.0 fusion.107
  240.1 2.0 fusion.108
  242.1 25.6 %collective-permute-done.22 = bf16[1536,512]{1,0:T(8,128)(2,1)S(1)} collective-permute-done((bf16[1536,512]{1,0:T(8,128)(2,1)S(1)}, bf16[1536,512]{1,0:T(8,128)(2,1)S(1)}, u32[]{:S(2)}, u32[]{:S(2)}) %collective-permute-start.22) | collective-permute-done | bytes 1572896 | tf_op jit(solution)/shard_map/ppermute | solution.py:33
  267.7 2.0 fusion.109
  271.5 3.4 fusion.110
  298.1 2.0 fusion.104
  300.6 6.8 %broadcast_multiply_fusion = (f32[512,512]{1,0:T(8,128)}, f32[512,512]{1,0:T(8,128)}, f32[512,512]{1,0:T(8,128)}, f32[512,512]{1,0:T(8,128)}, f32[512,512]{1,0:T(8,128)}, /*index=5*/f32[512,512]{1,0:T(8,128)}) fusion(f32[512]{0:T(512)S(1)} %copy-done.39, f32[]{:T(128)} %bitcast.13, f32[512,512]{1,0:T(8,128)} %fusion.110, ...), kind=kLoop, calls=%fused_computation.89 | loop fusion | flops 5242880 | bytes 18876440 | tf_op jit(solution)/shard_map/mul | solution.py:144
  307.4 2.6 copy.7
  309.9 2.5 copy.8
  312.5 2.5 copy.10
  315.0 2.6 copy.11
  317.6 2.5 copy.9
  320.1 2.5 copy.13
  322.6 2.6 fusion.111
  325.4 2.6 fusion.56
  328.1 2.7 fusion.52
  330.8 2.9 fusion.58
  333.7 3.1 fusion.28
  336.7 3.0 copy.6
  341.0 3.6 convolution_add_fusion.3
  344.7 2.9 fusion.61
  352.7 3.2 fusion.23
  355.9 9.0 %copy.15 = f32[1536,1,512]{2,1,0:T(1,128)} copy(f32[1536,1,512]{2,0,1:T(8,128)S(1)} %fusion.23) | data formatting | bytes 6291456 | tf_op jit(solution)/shard_map/reshape | solution.py:146
  (140 shorter events, 33.4 us)
Async XLA Ops:
  0.0 29.2 %collective-permute-start.1 = (bf16[384,1536]{1,0:T(8,128)(2,1)}, bf16[384,1536]{1,0:T(8,128)(2,1)S(1)}, u32[]{:S(2)}, u32[]{:S(2)}) collective-permute-start(bf16[384,1536]{1,0:T(8,128)(2,1)} %param.8), channel_id=1, source_target_pairs={{0,4},{2,6},{4,0},{6,2},{8,12},{10,14},{12,8},{14,10},{1,5},{3,7},... | collective-permute-start | bytes 3538952 | tf_op jit(solution)/shard_map/ppermute | solution.py:33
  3.1 28.8 %collective-permute-start = (bf16[384,1536]{1,0:T(8,128)(2,1)}, bf16[384,1536]{1,0:T(8,128)(2,1)S(1)}, u32[]{:S(2)}, u32[]{:S(2)}) collective-permute-start(bf16[384,1536]{1,0:T(8,128)(2,1)} %param.8), channel_id=1, source_target_pairs={{0,2},{2,0},{4,6},{6,4},{8,10},{10,8},{12,14},{14,12},{1,3},{3,1},... | collective-permute-start | bytes 3538952 | tf_op jit(solution)/shard_map/ppermute | solution.py:33
  29.2 15.7 %copy-start.32 = (bf16[384,1536]{1,0:T(8,128)(2,1)}, bf16[384,1536]{1,0:T(8,128)(2,1)S(1)}, u32[]{:S(2)}) copy-start(bf16[384,1536]{1,0:T(8,128)(2,1)S(1)} %collective-permute-done.1) | copy-start | bytes 3538948
  30.1 14.7 %collective-permute-start.2 = (bf16[192,1536]{1,0:T(8,128)(2,1)}, bf16[192,1536]{1,0:T(8,128)(2,1)S(1)}, u32[]{:S(2)}, u32[]{:S(2)}) collective-permute-start(bf16[192,1536]{1,0:T(8,128)(2,1)} %slice.12), channel_id=1, source_target_pairs={{0,2},{2,0},{4,6},{6,4},{8,10},{10,8},{12,14},{14,12},{1,3},{3,1},... | collective-permute-start | bytes 1769480 | tf_op jit(solution)/shard_map/ppermute | solution.py:33
  31.8 15.2 %copy-start.34 = (bf16[384,1536]{1,0:T(8,128)(2,1)}, bf16[384,1536]{1,0:T(8,128)(2,1)S(1)}, u32[]{:S(2)}) copy-start(bf16[384,1536]{1,0:T(8,128)(2,1)S(1)} %collective-permute-done) | copy-start | bytes 3538948
  32.7 14.2 %collective-permute-start.3 = (bf16[192,1536]{1,0:T(8,128)(2,1)}, bf16[192,1536]{1,0:T(8,128)(2,1)}, u32[]{:S(2)}, u32[]{:S(2)}) collective-permute-start(bf16[192,1536]{1,0:T(8,128)(2,1)} %slice.13), channel_id=1, source_target_pairs={{0,4},{2,6},{4,0},{6,2},{8,12},{10,14},{12,8},{14,10},{1,5},{3,7},... | collective-permute-start | bytes 1769480 | tf_op jit(solution)/shard_map/ppermute | solution.py:33
  34.3 22.0 %collective-permute-start.4 = (bf16[384,1536]{1,0:T(8,128)(2,1)}, bf16[384,1536]{1,0:T(8,128)(2,1)}, u32[]{:S(2)}, u32[]{:S(2)}) collective-permute-start(bf16[384,1536]{1,0:T(8,128)(2,1)} %param.8), channel_id=1, source_target_pairs={{4,8},{6,10},{9,5},{11,7},{20,24},{22,26},{25,21},{27,23}} | collective-permute-start | bytes 3538952 | tf_op jit(solution)/shard_map/ppermute | solution.py:50
  50.5 2.9 copy-start.9
  50.5 52.2 %copy-start.6 = (bf16[384,1536]{1,0:T(8,128)(2,1)}, bf16[384,1536]{1,0:T(8,128)(2,1)S(1)}, u32[]{:S(2)}) copy-start(bf16[384,1536]{1,0:T(8,128)(2,1)S(1)} %get-tuple-element.35) | copy-start | bytes 3538948
  53.4 49.3 %collective-permute-start.10 = (bf16[1536,1536]{1,0:T(8,128)(2,1)}, bf16[1536,1536]{1,0:T(8,128)(2,1)}, u32[]{:S(2)}, u32[]{:S(2)}) collective-permute-start(bf16[1536,1536]{1,0:T(8,128)(2,1)} %pad_maximum_fusion), channel_id=1, source_target_pairs={{1,0},{3,2},{5,4},{7,6},{8,9},{10,11},{12,13},{14,15},{17,16},{19,... | collective-permute-start | bytes 14155784 | tf_op jit(solution)/shard_map/ppermute | solution.py:100
  54.6 3.4 collective-permute-start.7
  56.3 3.4 collective-permute-start.5
  58.0 5.8 %collective-permute-start.8 = (bf16[384,1536]{1,0:T(8,128)(2,1)}, bf16[384,1536]{1,0:T(8,128)(2,1)}, u32[]{:S(2)}, u32[]{:S(2)}) collective-permute-start(bf16[384,1536]{1,0:T(8,128)(2,1)} %collective-permute-done.7), channel_id=1, source_target_pairs={{5,1},{7,3},{8,12},{10,14},{21,17},{23,19},{24,28},{26,30}} | collective-permute-start | bytes 3538952 | tf_op jit(solution)/shard_map/ppermute | solution.py:50
  62.1 33.9 %collective-permute-start.6 = (bf16[384,1536]{1,0:T(8,128)(2,1)}, bf16[384,1536]{1,0:T(8,128)(2,1)}, u32[]{:S(2)}, u32[]{:S(2)}) collective-permute-start(bf16[384,1536]{1,0:T(8,128)(2,1)} %broadcast_select_fusion.4), channel_id=1, source_target_pairs={{1,3},{3,1},{5,7},{7,5},{8,10},{10,8},{12,14},{14,12},{17,19},{19,... | collective-permute-start | bytes 3538952 | tf_op jit(solution)/shard_map/ppermute | solution.py:50
  66.2 33.1 %collective-permute-start.9 = (bf16[384,1536]{1,0:T(8,128)(2,1)}, bf16[384,1536]{1,0:T(8,128)(2,1)}, u32[]{:S(2)}, u32[]{:S(2)}) collective-permute-start(bf16[384,1536]{1,0:T(8,128)(2,1)} %broadcast_select_fusion.3), channel_id=1, source_target_pairs={{1,3},{3,1},{5,7},{7,5},{8,10},{10,8},{12,14},{14,12},{17,19},{19,... | collective-permute-start | bytes 3538952 | tf_op jit(solution)/shard_map/ppermute | solution.py:50
  67.9 38.5 %collective-permute-start.11 = (bf16[1536,512]{1,0:T(8,128)(2,1)}, bf16[1536,512]{1,0:T(8,128)(2,1)}, u32[]{:S(2)}, u32[]{:S(2)}) collective-permute-start(bf16[1536,512]{1,0:T(8,128)(2,1)} %bitcast), channel_id=1, source_target_pairs={{0,1},{1,0},{2,3},{3,2},{4,5},{5,4},{6,7},{7,6},{8,9},{9,8},{10,11... | collective-permute-start | bytes 4718600 | tf_op jit(solution)/shard_map/ppermute | solution.py:14
  99.3 3.4 copy-start.8
  99.3 3.4 copy-start.10
  119.8 14.5 %collective-permute-start.19 = (bf16[1536,512]{1,0:T(8,128)(2,1)S(1)}, bf16[1536,512]{1,0:T(8,128)(2,1)S(1)}, u32[]{:S(2)}, u32[]{:S(2)}) collective-permute-start(bf16[1536,512]{1,0:T(8,128)(2,1)S(1)} %fusion.25), channel_id=1, source_target_pairs={{4,8},{6,10},{8,4},{10,6},{5,9},{7,11},{9,5},{11,7},{20,24},{22,26... | collective-permute-start | bytes 4718600 | tf_op jit(solution)/shard_map/ppermute | solution.py:33
  120.5 45.8 %collective-permute-start.15 = (bf16[1536,512]{1,0:T(8,128)(2,1)S(1)}, bf16[1536,512]{1,0:T(8,128)(2,1)S(1)}, u32[]{:S(2)}, u32[]{:S(2)}) collective-permute-start(bf16[1536,512]{1,0:T(8,128)(2,1)S(1)} %fusion.25), channel_id=1, source_target_pairs={{0,4},{2,6},{4,0},{6,2},{8,12},{10,14},{12,8},{14,10},{1,5},{3,7},... | collective-permute-start | bytes 4718600 | tf_op jit(solution)/shard_map/ppermute | solution.py:33
  134.3 67.0 %collective-permute-start.20 = (bf16[1536,512]{1,0:T(8,128)(2,1)S(1)}, bf16[1536,512]{1,0:T(8,128)(2,1)S(1)}, u32[]{:S(2)}, u32[]{:S(2)}) collective-permute-start(bf16[1536,512]{1,0:T(8,128)(2,1)S(1)} %collective-permute-done.19), channel_id=1, source_target_pairs={{4,0},{6,2},{8,12},{10,14},{5,1},{7,3},{9,13},{11,15},{20,16},{22,... | collective-permute-start | bytes 4718600 | tf_op jit(solution)/shard_map/ppermute | solution.py:33
  166.3 39.2 %copy-start.17 = (bf16[1536,512]{1,0:T(8,128)(2,1)}, bf16[1536,512]{1,0:T(8,128)(2,1)S(1)}, u32[]{:S(2)}) copy-start(bf16[1536,512]{1,0:T(8,128)(2,1)S(1)} %collective-permute-done.15) | copy-start | bytes 4718596
  166.3 35.8 %collective-permute-start.24 = (bf16[1536,512]{1,0:T(8,128)(2,1)S(1)}, bf16[1536,512]{1,0:T(8,128)(2,1)S(1)}, u32[]{:S(2)}, u32[]{:S(2)}) collective-permute-start(bf16[1536,512]{1,0:T(8,128)(2,1)S(1)} %collective-permute-done.15), channel_id=1, source_target_pairs={{4,8},{6,10},{8,4},{10,6},{5,9},{7,11},{9,5},{11,7},{20,24},{22,26... | collective-permute-start | bytes 4718600 | tf_op jit(solution)/shard_map/ppermute | solution.py:33
  167.1 37.3 %collective-permute-start.13 = (bf16[1536,512]{1,0:T(8,128)(2,1)S(1)}, bf16[1536,512]{1,0:T(8,128)(2,1)S(1)}, u32[]{:S(2)}, u32[]{:S(2)}) collective-permute-start(bf16[1536,512]{1,0:T(8,128)(2,1)S(1)} %fusion.25), channel_id=1, source_target_pairs={{0,2},{2,0},{4,6},{6,4},{8,10},{10,8},{12,14},{14,12},{1,3},{3,1},... | collective-permute-start | bytes 4718600 | tf_op jit(solution)/shard_map/ppermute | solution.py:33
  167.6 70.5 %collective-permute-start.17 = (bf16[1536,512]{1,0:T(8,128)(2,1)S(1)}, bf16[1536,512]{1,0:T(8,128)(2,1)S(1)}, u32[]{:S(2)}, u32[]{:S(2)}) collective-permute-start(bf16[1536,512]{1,0:T(8,128)(2,1)S(1)} %collective-permute-done.15), channel_id=1, source_target_pairs={{0,2},{2,0},{4,6},{6,4},{8,10},{10,8},{12,14},{14,12},{1,3},{3,1},... | collective-permute-start | bytes 4718600 | tf_op jit(solution)/shard_map/ppermute | solution.py:33
  201.5 66.2 %collective-permute-start.22 = (bf16[1536,512]{1,0:T(8,128)(2,1)S(1)}, bf16[1536,512]{1,0:T(8,128)(2,1)S(1)}, u32[]{:S(2)}, u32[]{:S(2)}) collective-permute-start(bf16[1536,512]{1,0:T(8,128)(2,1)S(1)} %broadcast_select_fusion.2), channel_id=1, source_target_pairs={{0,2},{2,0},{4,6},{6,4},{8,10},{10,8},{12,14},{14,12},{1,3},{3,1},... | collective-permute-start | bytes 4718600 | tf_op jit(solution)/shard_map/ppermute | solution.py:33
  202.1 67.6 %collective-permute-start.25 = (bf16[1536,512]{1,0:T(8,128)(2,1)S(1)}, bf16[1536,512]{1,0:T(8,128)(2,1)S(1)}, u32[]{:S(2)}, u32[]{:S(2)}) collective-permute-start(bf16[1536,512]{1,0:T(8,128)(2,1)S(1)} %collective-permute-done.24), channel_id=1, source_target_pairs={{4,0},{6,2},{8,12},{10,14},{5,1},{7,3},{9,13},{11,15},{20,16},{22,... | collective-permute-start | bytes 4718600 | tf_op jit(solution)/shard_map/ppermute | solution.py:33
  205.5 69.4 %collective-permute-start.14 = (f32[512,512]{1,0:T(8,128)S(1)}, f32[512,512]{1,0:T(8,128)S(1)}, u32[]{:S(2)}, u32[]{:S(2)}) collective-permute-start(f32[512,512]{1,0:T(8,128)S(1)} %fusion.105), channel_id=1, source_target_pairs={{0,1},{1,0},{2,3},{3,2},{4,5},{5,4},{6,7},{7,6},{8,9},{9,8},{10,11... | collective-permute-start | bytes 3145736 | tf_op jit(solution)/shard_map/ppermute | solution.py:14
  206.5 33.5 %copy-start.29 = (f32[512,512]{1,0:T(8,128)}, f32[512,512]{1,0:T(8,128)S(1)}, u32[]{:S(2)}) copy-start(f32[512,512]{1,0:T(8,128)S(1)} %fusion.106) | copy-start | bytes 3145732
  206.6 68.4 %collective-permute-start.16 = (f32[512,512]{1,0:T(8,128)S(1)}, f32[512,512]{1,0:T(8,128)S(1)}, u32[]{:S(2)}, u32[]{:S(2)}) collective-permute-start(f32[512,512]{1,0:T(8,128)S(1)} %fusion.106), channel_id=1, source_target_pairs={{0,1},{1,0},{2,3},{3,2},{4,5},{5,4},{6,7},{7,6},{8,9},{9,8},{10,11... | collective-permute-start | bytes 3145736 | tf_op jit(solution)/shard_map/ppermute | solution.py:14
  240.1 60.0 %collective-permute-start.18 = (f32[512,512]{1,0:T(8,128)}, f32[512,512]{1,0:T(8,128)}, u32[]{:S(2)}, u32[]{:S(2)}) collective-permute-start(f32[512,512]{1,0:T(8,128)} %fusion.107), channel_id=1, source_target_pairs={{0,1},{1,0},{2,3},{3,2},{4,5},{5,4},{6,7},{7,6},{8,9},{9,8},{10,11... | collective-permute-start | bytes 3145736 | tf_op jit(solution)/shard_map/ppermute | solution.py:14
  267.7 32.4 %collective-permute-start.21 = (f32[512,512]{1,0:T(8,128)}, f32[512,512]{1,0:T(8,128)}, u32[]{:S(2)}, u32[]{:S(2)}) collective-permute-start(f32[512,512]{1,0:T(8,128)} %fusion.108), channel_id=1, source_target_pairs={{0,1},{1,0},{2,3},{3,2},{4,5},{5,4},{6,7},{7,6},{8,9},{9,8},{10,11... | collective-permute-start | bytes 3145736 | tf_op jit(solution)/shard_map/ppermute | solution.py:14
  269.7 30.4 %collective-permute-start.23 = (f32[512,512]{1,0:T(8,128)}, f32[512,512]{1,0:T(8,128)}, u32[]{:S(2)}, u32[]{:S(2)}) collective-permute-start(f32[512,512]{1,0:T(8,128)} %fusion.109), channel_id=1, source_target_pairs={{0,1},{1,0},{2,3},{3,2},{4,5},{5,4},{6,7},{7,6},{8,9},{9,8},{10,11... | collective-permute-start | bytes 3145736 | tf_op jit(solution)/shard_map/ppermute | solution.py:14
  271.5 5.9 %copy-start.40 = (f32[8]{0:T(128)S(1)}, f32[8]{0:T(128)}, u32[]{:S(2)}) copy-start(f32[8]{0:T(128)} %param.9) | copy-start | bytes 100
  271.5 15.4 %copy-start.41 = (s32[8,3,2]{0,2,1:T(2,128)S(1)}, s32[8,3,2]{0,2,1:T(2,128)}, u32[]{:S(2)}) copy-start(s32[8,3,2]{0,2,1:T(2,128)} %param.11) | copy-start | bytes 580
  274.9 25.2 %collective-permute-start.26 = (f32[512,512]{1,0:T(8,128)}, f32[512,512]{1,0:T(8,128)}, u32[]{:S(2)}, u32[]{:S(2)}) collective-permute-start(f32[512,512]{1,0:T(8,128)} %fusion.110), channel_id=1, source_target_pairs={{0,1},{1,0},{2,3},{3,2},{4,5},{5,4},{6,7},{7,6},{8,9},{9,8},{10,11... | collective-permute-start | bytes 3145736 | tf_op jit(solution)/shard_map/ppermute | solution.py:14
  276.9 45.8 %collective-permute-start.27 = (bf16[1536,512]{1,0:T(8,128)(2,1)}, bf16[1536,512]{1,0:T(8,128)(2,1)}, u32[]{:S(2)}, u32[]{:S(2)}) collective-permute-start(bf16[1536,512]{1,0:T(8,128)(2,1)} %broadcast_select_fusion.1), channel_id=1, source_target_pairs={{0,2},{2,0},{4,6},{6,4},{8,10},{10,8},{12,14},{14,12},{1,3},{3,1},... | collective-permute-start | bytes 4718600 | tf_op jit(solution)/shard_map/ppermute | solution.py:33
  300.1 33.6 %collective-permute-start.12 = (f32[512,512]{1,0:T(8,128)}, f32[512,512]{1,0:T(8,128)}, u32[]{:S(2)}, u32[]{:S(2)}) collective-permute-start(f32[512,512]{1,0:T(8,128)} %fusion.104), channel_id=1, source_target_pairs={{0,1},{1,0},{2,3},{3,2},{4,5},{5,4},{6,7},{7,6},{8,9},{9,8},{10,11... | collective-permute-start | bytes 3145736 | tf_op jit(solution)/shard_map/ppermute | solution.py:14
  325.2 8.5 %collective-permute-start.28 = (f32[512,512]{1,0:T(8,128)S(1)}, f32[512,512]{1,0:T(8,128)S(1)}, u32[]{:S(2)}, u32[]{:S(2)}) collective-permute-start(f32[512,512]{1,0:T(8,128)S(1)} %fusion.111), channel_id=1, source_target_pairs={{0,1},{1,0},{2,3},{3,2},{4,5},{5,4},{6,7},{7,6},{8,9},{9,8},{10,11... | collective-permute-start | bytes 3145736 | tf_op jit(solution)/shard_map/ppermute | solution.py:14
  336.7 4.3 %copy-start.16 = (f32[512,512]{1,0:T(8,128)}, f32[512,512]{1,0:T(8,128)S(1)}, u32[]{:S(2)}) copy-start(f32[512,512]{1,0:T(8,128)S(1)} %get-tuple-element.49) | copy-start | bytes 3145732
  341.0 3.6 copy-start.26
  344.7 2.9 copy-start.12
  344.7 2.9 copy-start.18
  344.7 2.9 copy-start.22
  347.6 2.8 copy-start.1
  347.6 3.1 copy-start.11
  347.6 3.5 copy-start.20
  347.7 3.8 %copy-start.21 = (f32[512,512]{0,1:T(8,128)S(1)}, f32[512,512]{0,1:T(8,128)}, u32[]{:S(2)}) copy-start(f32[512,512]{0,1:T(8,128)} %copy.9) | copy-start | bytes 3145732
  (23 other events, 48.6 us)
